TPU v7x, 256 devices: a whole 4x4x8 slice. The times are simulated.
256 devices in a mesh: ens: 16 (over x_hi, z), lon: 4 (over x_lo, core), lat: 4 (over y).
Axes of the slice: x: 4 (x_hi: 2, x_lo: 2; x = x_hi * 2 + x_lo), y: 4, z: 8, core: 2. Of those that a mesh axis runs over, the one named last changes fastest.
Arguments:
- members: float32 [16, 80, 32, 640], P('ens', 'lat', 'lon'), may hold values from -6 to 6
- analysis: float32 [80, 32, 640], P('lat', 'lon', 'ens'), may hold values from -6 to 6
- stencils: float32 [7, 7, 7, 80], replicated, may hold values from -0.84 to 0.84
- mixing: float32 [7, 640, 640], replicated, may hold values from -0.09375 to 0.09375
Outputs:
- members_grad: float32 [16, 80, 32, 640], P('ens', 'lat', 'lon')
- crps_field: float32 [80, 32, 640], P('lat', 'lon', 'ens')
All inputs are finite; a program needn't handle non-finite values.
Results may differ from a plain program's by a relative error of at most 0.00016.
Values sent between devices are 32-bit elements; how exact they have to be, the bound alone decides.
A program may use at most 128 MiB of HBM per device.

v0:
```python
import jax
import jax.numpy as jnp
from jax import lax
from jax.sharding import PartitionSpec as P

BASES = 7
SPAN = 7
smooth = 0.01
highest = lax.Precision.HIGHEST


def extended_2(block, sides, width, periodic):
    for axis, dim in sides:
        count = lax.axis_size(axis)
        forward = [(i, i + 1) for i in range(count - 1)]
        if periodic:
            forward.append((count - 1, 0))
        backward = [(target, source) for source, target in forward]
        low = lax.ppermute(
            lax.slice_in_dim(block, block.shape[dim] - width, None, axis=dim), axis, forward
        )
        high = lax.ppermute(lax.slice_in_dim(block, 0, width, axis=dim), axis, backward)
        block = jnp.concatenate([low, block, high], axis=dim)
    return block


def extend(field_block):
    margin = SPAN // 2
    widened = extended_2(field_block, (("lon", 2),), margin, True)
    return extended_2(widened, (("lat", 1),), margin, False)


def apply_taps(extended, weights, height, breadth):
    running = jnp.zeros(
        (weights.shape[0], extended.shape[0], height, breadth, extended.shape[3]), jnp.float32
    )
    for row_tap in range(SPAN):
        for col_tap in range(SPAN):
            tap_index = row_tap * SPAN + col_tap
            running = (
                running
                + weights[:, tap_index, None, :, None, None]
                * extended[None, :, row_tap : row_tap + height, col_tap : col_tap + breadth, :]
            )
    return jnp.transpose(running, (1, 2, 3, 0, 4))


def local(members, analysis, stencils, mixing):
    own_count, height, breadth, channels = members.shape
    margin = SPAN // 2
    first_row = lax.axis_index("lat") * height
    padded = jnp.pad(stencils, ((0, 0), (0, 0), (0, 0), (margin, margin)))
    window = lax.dynamic_slice_in_dim(padded, first_row, height + 2 * margin, 3)
    forward = window[:, :, :, margin : margin + height].reshape(BASES, SPAN * SPAN, height)
    backward = jnp.stack(
        [
            window[:, SPAN - 1 - row_tap, ::-1, row_tap : row_tap + height]
            for row_tap in range(SPAN)
        ],
        axis=1,
    ).reshape(BASES, SPAN * SPAN, height)
    stencilled = apply_taps(extend(members), forward, height, breadth)
    mixed = jnp.dot(
        stencilled.reshape(-1, BASES * channels),
        mixing.reshape(BASES * channels, channels),
        precision=highest,
        preferred_element_type=jnp.float32,
    )
    bounded_activation = jnp.tanh(mixed.reshape(own_count, height, breadth, channels))
    predicted_fields = members + bounded_activation
    observed_truth = lax.all_gather(analysis, "ens", axis=2, tiled=True)
    prediction_error = predicted_fields - observed_truth[None]
    differ = (
        prediction_error[:, None]
        - lax.all_gather(prediction_error, "ens", axis=0, tiled=True)[None]
    )
    smooth_abs = jnp.sqrt(differ * differ + smooth)
    sum_abs = jnp.sum(smooth_abs, 1)
    sum_slope = jnp.sum(differ / smooth_abs, 1)
    members_total = own_count * lax.axis_size("ens")
    own_abs = jnp.sqrt(prediction_error * prediction_error + smooth)
    partial_score_sums = jnp.sum(
        own_abs / members_total - sum_abs / (2.0 * members_total * (members_total - 1)), 0
    )
    crps_field = lax.psum_scatter(partial_score_sums, "ens", scatter_dimension=2, tiled=True)
    grad_out = prediction_error / own_abs - sum_slope / (members_total - 1.0)
    inner_grad = grad_out * (1.0 - bounded_activation * bounded_activation)
    spread = apply_taps(extend(inner_grad), backward, height, breadth)
    adjoint = lax.dot_general(
        spread.reshape(-1, BASES, channels),
        mixing,
        (((1, 2), (0, 2)), ((), ())),
        precision=highest,
        preferred_element_type=jnp.float32,
    )
    members_grad = grad_out + adjoint.reshape(own_count, height, breadth, channels)
    return (members_grad, crps_field)


def solution(mesh):
    in_specs = (P("ens", "lat", "lon", None), P("lat", "lon", "ens"), P(), P())
    out_specs = (P("ens", "lat", "lon", None), P("lat", "lon", "ens"))
    return jax.shard_map(local, mesh=mesh, in_specs=in_specs, out_specs=out_specs, check_vma=False)
```

profile of v0, /device:TPU:8, one launch (start us, length us, event | category | flops | bytes accessed | tf_op | source)
XLA Modules:
  0.0 509.7 jit_solution(6073563373159299852)
XLA Ops:
  7.2 2.0 fusion.228
  9.2 1.7 collective-permute-start.1
  10.9 1.0 pad_dynamic-slice_fusion.6
  12.1 1.7 copy.254
  16.7 0.7 copy.205
  18.1 0.7 copy.234
  37.3 0.7 copy.242
  42.1 62.8 %all_gather.6 = f32[20,8,640]{0,1,2:T(8,128)S(1)} all-gather(f32[20,8,40]{0,1,2:T(8,128)} %copy.254), channel_id=1, replica_groups=mesh['ens'=16,'lon'=4,'lat'=4] {'ens'}, dimensions={2}, use_global_device_ids=true | all-gather | bytes 435200 | tf_op jit(solution)/shard_map/all_gather | solution.py:71
  104.8 1.7 copy.255
  106.6 3.5 collective-permute-start.2
  110.1 2.4 collective-permute-start.3
  113.4 3.5 collective-permute-done.3
  117.0 1.5 slice_bitcast_fusion.86
  119.0 3.3 slice_bitcast_fusion.62
  122.7 18.8 %multiply_add_fusion = f32[7,1,20,8,640]{4,3,0,2,1:T(8,128)S(1)} fusion(f32[20,8,640]{2,1,0:T(8,128)} %get-tuple-element.68, f32[7,20]{0,1:T(8,128)S(1)} %copy-done.36, f32[20,8,640]{2,1,0:T(8,128)} %get-tuple-element.69, f32[7,20]{0,1:T(8,128)S(1)} %copy-done.37, f32[20,8,640]{2,1,0:T(8,128)} %get-tuple-element.70, f32[7,20]{0,1:T(8,128)S(1)} %copy-done.38, ...), kind=kLoop, calls=%fused_computation.104 | loop fusion | flops 69529600 | bytes 22965040 | tf_op jit(solution)/shard_map/add | solution.py:41
  141.5 8.8 %bitcast_subtract_fusion.2 = (f32[1,20,8,640]{3,2,1,0:T(8,128)}, f32[20,8,640]{2,1,0:T(8,128)S(1)}) fusion(f32[20,8,640]{2,1,0:T(8,128)S(1)} %copy-done.3, f32[1,20,8,640]{3,2,1,0:T(8,128)S(1)} %copy-done, f32[20,8,4480]{2,1,0:T(8,128)S(1)} %bitcast.460, f32[4480,640,1]{1,0,2:T(8,128)S(1)} %bitcast.457), kind=kOutput, calls=%fused_computation.331 | convolution fusion | flops 5505228800 | bytes 15974400 | tf_op jit(solution)/shard_map/dot_general | solution.py:63
  152.3 110.2 %all-gather.2.cloned.1.call-done = f32[16,20,8,640]{3,2,1,0:T(8,128)} async-done(((f32[1,20,8,640]{3,2,1,0:T(8,128)}), f32[16,20,8,640]{3,2,1,0:T(8,128)}) %all-gather.2.cloned.1.call-update) | async-done | bytes 6553616 | tf_op jit(solution)/shard_map/all_gather | solution.py:75
  262.5 6.4 %fusion.2 = (f32[20,8,640]{2,1,0:T(8,128)S(1)}, f32[20,8,640]{2,1,0:T(8,128)S(1)}) fusion(f32[16,20,8,640]{3,2,1,0:T(8,128)} %all-gather.2.cloned.1.call-done, f32[20,8,640]{2,1,0:T(8,128)S(1)} %bitcast.461), kind=kLoop, calls=%fused_computation.3 | loop fusion | flops 9625600 | bytes 7782400 | tf_op jit(solution)/shard_map/reduce_sum | solution.py:78
  269.7 1.4 collective-permute-start.5
  290.6 4.9 copy.307
  295.6 5.6 %reshape.1431 = f32[640,160]{1,0:T(8,128)} reshape(f32[640,20,8]{2,1,0:T(8,128)} %bitcast.452) | data formatting | bytes 819200
  301.2 3.4 collective-permute-start.6
  304.6 2.5 collective-permute-start.7
  308.0 3.4 collective-permute-done.7
  311.6 3.2 slice_bitcast_fusion.20
  314.8 0.8 slice_bitcast_fusion.40
  315.7 3.9 slice_bitcast_fusion.41
  319.7 20.4 %fusion.234 = f32[20,8,7,640]{3,1,2,0:T(8,128)S(1)} fusion(f32[20,8,640]{2,1,0:T(8,128)} %get-tuple-element.26, f32[7,20]{0,1:T(8,128)} %copy.305, f32[20,8,640]{2,1,0:T(8,128)} %get-tuple-element.27, f32[7,20]{0,1:T(8,128)} %copy.304, f32[20,8,640]{2,1,0:T(8,128)} %get-tuple-element.28, f32[7,20]{0,1:T(8,128)} %copy.303, ...), kind=kLoop, calls=%fused_computation.6.clone.clone.clone.clone.clone.1 | loop fusion | flops 69529600 | bytes 22965040 | tf_op jit(solution)/shard_map/dot_general | solution.py:89
  340.2 12.2 %fusion.206 = f32[1,20,8,640]{3,2,1,0:T(8,128)} fusion(f32[7,640,640]{2,1,0:T(8,128)S(1)} %bitcast.459, f32[20,8,640]{2,1,0:T(8,128)S(1)} %copy-done.7, f32[1,20,8,640]{3,2,1,0:T(8,128)S(1)} %copy-done.1, f32[20,8,7,640]{3,1,2,0:T(8,128)S(1)} %fusion.234), kind=kOutput, calls=%fused_computation.205 | convolution fusion | flops 5505638400 | bytes 15564800 | tf_op jit(solution)/shard_map/dot_general | solution.py:89
  352.4 148.5 %reduce-scatter.4.cloned.1.call-done = f32[40,160]{1,0:T(8,128)} async-done(((f32[640,160]{1,0:T(8,128)}), f32[40,160]{1,0:T(8,128)}) %reduce-scatter.4.cloned.1.call-update) | async-done | bytes 25616
  500.9 0.9 reshape.1432
  501.8 0.8 copy.308
  (253 shorter events, 51.0 us)
Async XLA Ops:
  7.2 255.4 %all-gather.2.cloned.1.call-start = ((), (), s32[]{:S(2)}) async-start(), calls=%async_computation.1 | async-start | bytes 6963200 | tf_op jit(solution)/shard_map/all_gather | solution.py:75
  9.2 97.3 %collective-permute-start = (f32[1,20,3,640]{3,2,1,0:T(4,128)}, f32[1,20,3,640]{3,2,1,0:T(4,128)S(1)}, u32[]{:S(2)}, u32[]{:S(2)}) collective-permute-start(f32[1,20,3,640]{3,2,1,0:T(4,128)} %get-tuple-element.116), channel_id=1, source_target_pairs={{0,4},{4,8},{8,12},{12,0},{1,5},{5,9},{9,13},{13,1},{2,6},{6,10},{... | collective-permute-start | bytes 460808 | tf_op jit(solution)/shard_map/ppermute | solution.py:19
  9.2 97.3 %collective-permute-start.1 = (f32[1,20,3,640]{3,2,1,0:T(4,128)}, f32[1,20,3,640]{3,2,1,0:T(4,128)S(1)}, u32[]{:S(2)}, u32[]{:S(2)}) collective-permute-start(f32[1,20,3,640]{3,2,1,0:T(4,128)} %get-tuple-element.117), channel_id=1, source_target_pairs={{4,0},{8,4},{12,8},{0,12},{5,1},{9,5},{13,9},{1,13},{6,2},{10,6},{... | collective-permute-start | bytes 460808 | tf_op jit(solution)/shard_map/ppermute | solution.py:22
  42.1 64.5 %copy-start = (f32[1,20,8,640]{3,2,1,0:T(8,128)S(1)}, f32[1,20,8,640]{3,2,1,0:T(8,128)}, u32[]{:S(2)}) copy-start(f32[1,20,8,640]{3,2,1,0:T(8,128)} %param.4) | copy-start | bytes 1228804
  106.6 6.8 %collective-permute-start.2 = (f32[1,3,14,640]{3,2,1,0:T(8,128)S(1)}, f32[1,3,14,640]{3,2,1,0:T(8,128)S(1)}, u32[]{:S(2)}, u32[]{:S(2)}) collective-permute-start(f32[1,3,14,640]{3,2,1,0:T(8,128)S(1)} %get-tuple-element.94), channel_id=1, source_target_pairs={{0,1},{1,2},{2,3},{4,5},{5,6},{6,7},{8,9},{9,10},{10,11},{12,13},{... | collective-permute-start | bytes 322568 | tf_op jit(solution)/shard_map/ppermute | solution.py:19
  110.1 6.8 %collective-permute-start.3 = (f32[1,3,14,640]{3,2,1,0:T(8,128)S(1)}, f32[1,3,14,640]{3,2,1,0:T(8,128)S(1)}, u32[]{:S(2)}, u32[]{:S(2)}) collective-permute-start(f32[1,3,14,640]{3,2,1,0:T(8,128)S(1)} %get-tuple-element.95), channel_id=1, source_target_pairs={{1,0},{2,1},{3,2},{5,4},{6,5},{7,6},{9,8},{10,9},{11,10},{13,12},{... | collective-permute-start | bytes 322568 | tf_op jit(solution)/shard_map/ppermute | solution.py:22
  118.6 3.6 copy-start.4
  118.7 3.6 copy-start.5
  118.7 3.6 copy-start.8
  118.7 3.6 copy-start.9
  118.7 3.6 copy-start.10
  122.3 19.2 %slice-start = ((s8[11468800]{0:T(1024)(128)(4,1)}), s8[4194304]{0:T(1024)(128)(4,1)S(1)}, s32[]{:S(2)}) async-start(s8[11468800]{0:T(1024)(128)(4,1)} %bitcast.455), calls=%async_computation.3 | async-start | bytes 8388608
  122.6 18.9 %slice-start.1 = ((s8[11468800]{0:T(1024)(128)(4,1)}), s8[4194304]{0:T(1024)(128)(4,1)S(1)}, s32[]{:S(2)}) async-start(s8[11468800]{0:T(1024)(128)(4,1)} %bitcast.455), calls=%async_computation.4 | async-start | bytes 8388608
  122.7 18.9 %slice-start.2 = ((s8[11468800]{0:T(1024)(128)(4,1)}), s8[3080192]{0:T(1024)(128)(4,1)S(1)}, s32[]{:S(2)}) async-start(s8[11468800]{0:T(1024)(128)(4,1)} %bitcast.455), calls=%async_computation.5 | async-start | bytes 6160384
  122.7 18.9 %copy-start.3 = (f32[20,8,640]{2,1,0:T(8,128)S(1)}, f32[20,8,640]{2,1,0:T(8,128)}, u32[]{:S(2)}) copy-start(f32[20,8,640]{2,1,0:T(8,128)} %copy.255) | copy-start | bytes 1228804
  141.5 9.1 %copy-start.2 = (f32[7,7,7,80]{3,2,1,0:T(8,128)S(1)}, f32[7,7,7,80]{3,2,1,0:T(8,128)}, u32[]{:S(2)}) copy-start(f32[7,7,7,80]{3,2,1,0:T(8,128)} %param.6) | copy-start | bytes 329284
  150.3 112.2 %copy-start.1 = (f32[1,20,8,640]{3,2,1,0:T(8,128)S(1)}, f32[1,20,8,640]{3,2,1,0:T(8,128)}, u32[]{:S(2)}) copy-start(f32[1,20,8,640]{3,2,1,0:T(8,128)} %get-tuple-element.222) | copy-start | bytes 1228804
  150.4 350.5 %reduce-scatter.4.cloned.1.call-start = ((), (), s32[]{:S(2)}) async-start(), calls=%async_computation.2 | async-start | bytes 696320
  269.3 31.8 %collective-permute-start.4 = (f32[1,20,3,640]{3,2,1,0:T(4,128)S(1)}, f32[1,20,3,640]{3,2,1,0:T(4,128)S(1)}, u32[]{:S(2)}, u32[]{:S(2)}) collective-permute-start(f32[1,20,3,640]{3,2,1,0:T(4,128)S(1)} %get-tuple-element.113), channel_id=1, source_target_pairs={{0,4},{4,8},{8,12},{12,0},{1,5},{5,9},{9,13},{13,1},{2,6},{6,10},{... | collective-permute-start | bytes 460808 | tf_op jit(solution)/shard_map/ppermute | solution.py:19
  269.7 31.4 %collective-permute-start.5 = (f32[1,20,3,640]{3,2,1,0:T(4,128)S(1)}, f32[1,20,3,640]{3,2,1,0:T(4,128)S(1)}, u32[]{:S(2)}, u32[]{:S(2)}) collective-permute-start(f32[1,20,3,640]{3,2,1,0:T(4,128)S(1)} %get-tuple-element.114), channel_id=1, source_target_pairs={{4,0},{8,4},{12,8},{0,12},{5,1},{9,5},{13,9},{1,13},{6,2},{10,6},{... | collective-permute-start | bytes 460808 | tf_op jit(solution)/shard_map/ppermute | solution.py:22
  301.2 6.8 %collective-permute-start.6 = (f32[1,3,14,640]{3,2,1,0:T(8,128)S(1)}, f32[1,3,14,640]{3,2,1,0:T(8,128)S(1)}, u32[]{:S(2)}, u32[]{:S(2)}) collective-permute-start(f32[1,3,14,640]{3,2,1,0:T(8,128)S(1)} %get-tuple-element.90), channel_id=1, source_target_pairs={{0,1},{1,2},{2,3},{4,5},{5,6},{6,7},{8,9},{9,10},{10,11},{12,13},{... | collective-permute-start | bytes 322568 | tf_op jit(solution)/shard_map/ppermute | solution.py:19
  304.6 6.8 %collective-permute-start.7 = (f32[1,3,14,640]{3,2,1,0:T(8,128)S(1)}, f32[1,3,14,640]{3,2,1,0:T(8,128)S(1)}, u32[]{:S(2)}, u32[]{:S(2)}) collective-permute-start(f32[1,3,14,640]{3,2,1,0:T(8,128)S(1)} %get-tuple-element.91), channel_id=1, source_target_pairs={{1,0},{2,1},{3,2},{5,4},{6,5},{7,6},{9,8},{10,9},{11,10},{13,12},{... | collective-permute-start | bytes 322568 | tf_op jit(solution)/shard_map/ppermute | solution.py:22
  315.7 4.0 copy-start.16
  315.7 4.0 copy-start.18
  315.7 4.0 copy-start.20
  315.7 4.0 copy-start.22
  315.7 4.0 copy-start.24
  315.7 4.0 copy-start.26
  315.7 24.5 %slice-start.3 = ((s8[11468800]{0:T(1024)(128)(4,1)}), s8[3080192]{0:T(1024)(128)(4,1)S(1)}, s32[]{:S(2)}) async-start(s8[11468800]{0:T(1024)(128)(4,1)} %bitcast.458), calls=%async_computation.6 | async-start | bytes 6160384
  315.7 24.5 %slice-start.4 = ((s8[11468800]{0:T(1024)(128)(4,1)}), s8[4194304]{0:T(1024)(128)(4,1)S(1)}, s32[]{:S(2)}) async-start(s8[11468800]{0:T(1024)(128)(4,1)} %bitcast.458), calls=%async_computation.7 | async-start | bytes 8388608
  319.7 20.5 %slice-start.5 = ((s8[11468800]{0:T(1024)(128)(4,1)}), s8[4194304]{0:T(1024)(128)(4,1)S(1)}, s32[]{:S(2)}) async-start(s8[11468800]{0:T(1024)(128)(4,1)} %bitcast.458), calls=%async_computation.8 | async-start | bytes 8388608
  319.7 20.5 %copy-start.7 = (f32[20,8,640]{2,1,0:T(8,128)S(1)}, f32[20,8,640]{2,1,0:T(8,128)}, u32[]{:S(2)}) copy-start(f32[20,8,640]{2,1,0:T(8,128)} %copy-done.6) | copy-start | bytes 1228804
  (32 other events, 113.4 us)
Sparse Core Ops, SparseCore 0:
  150.5 112.0 all-gather.1
  301.3 199.5 reduce-scatter.3
where the time goes:
time: 515 us; the launch traced here: 510 us
  waiting for transfers between devices  267 us (52%)
  local copies, waits for them, and re-layouts  81.7 us (16%)
  blocking collectives  62.8 us (12%)
  other arithmetic  46.9 us (9%)
  matrix products  21 us (4%)
  between operations  15.4 us (3%)
  starting transfers between devices  15.2 us (3%)
    unnamed x3, waiting for transfers between devices  149 us
    all_gather x1, waiting for transfers between devices, local(): lax.all_gather(prediction_error, 'ens', axis=0, tiled=True)[None]  110 us
    all_gather x1, blocking collectives, local(): observed_truth = lax.all_gather(analysis, 'ens', axis=2, tiled=True)  62.8 us
    mul x112, local copies, waits for them, and re-layouts, apply_taps(): weights[:, tap_index, None, :, None, None]  62 us
    dot_general x1, other arithmetic, local(): lax.dot_general(spread.reshape(-1, BASES, channels), mixing, (((1, 2), (0...  20.4 us
    add x1, other arithmetic, apply_taps(): running + weights[:, tap_index, None, :, None, None] * extended[None, :,...  18.8 us
    unnamed x119, local copies, waits for them, and re-layouts  14.5 us
    dot_general x1, matrix products, local(): lax.dot_general(spread.reshape(-1, BASES, channels), mixing, (((1, 2), (0...  12.2 us
  transfers between devices with their start and end apart: 10, of which 6 were waited for; matrix products, arithmetic and copies ran while one was open for 21% of the time, Pallas kernels for 0%

commit v1 on v0

--- a/solution.py
+++ b/solution.py
@@ -72,7 +72,10 @@
     prediction_error = predicted_fields - observed_truth[None]
     differ = (
         prediction_error[:, None]
-        - lax.all_gather(prediction_error, "ens", axis=0, tiled=True)[None]
+        - jnp.concatenate(
+            lax.all_to_all(jnp.stack([prediction_error] * lax.axis_size("ens")), "ens", 0, 0),
+            axis=0,
+        )[None]
     )
     smooth_abs = jnp.sqrt(differ * differ + smooth)
     sum_abs = jnp.sum(smooth_abs, 1)

time: 515 us -> 549 us (1.066)
  waiting for transfers between devices: 267 us -> 294 us
    all_to_all x0 -> x1, waiting for transfers between devices: none -> 136 us  [local(): lax.all_to_all(jnp.stack([prediction_error] * lax.axis_size('ens')), 'ens...]
    all_gather x1 -> x0, waiting for transfers between devices: 110 us -> none  [local(): lax.all_gather(prediction_error, 'ens', axis=0, tiled=True)[None]]
    unnamed x3 -> x2, waiting for transfers between devices: 149 us -> 150 us
    unnamed x119 -> x117, local copies, waits for them, and re-layouts: 14.5 us -> 14.5 us
  transfers between devices with their start and end apart: 10 -> 10, of which waited for: 6 -> 6; matrix products, arithmetic and copies ran while one was open for 21% -> 19% of each run, Pallas kernels for 0% -> 0%
where the time goes in v1:
time: 549 us; the launch traced here: 544 us
  waiting for transfers between devices  294 us (54%)
  local copies, waits for them, and re-layouts  85.3 us (16%)
  blocking collectives  62.8 us (11%)
  other arithmetic  46.6 us (8%)
  matrix products  20.2 us (4%)
  starting transfers between devices  20 us (4%)
  between operations  15.4 us (3%)
    unnamed x2, waiting for transfers between devices  150 us
    all_to_all x1, waiting for transfers between devices, local(): lax.all_to_all(jnp.stack([prediction_error] * lax.axis_size('ens')), 'ens...  136 us
    all_gather x1, blocking collectives, local(): observed_truth = lax.all_gather(analysis, 'ens', axis=2, tiled=True)  62.8 us
    mul x112, local copies, waits for them, and re-layouts, apply_taps(): weights[:, tap_index, None, :, None, None]  62 us
    dot_general x1, other arithmetic, local(): lax.dot_general(spread.reshape(-1, BASES, channels), mixing, (((1, 2), (0...  20.4 us
    add x1, other arithmetic, apply_taps(): running + weights[:, tap_index, None, :, None, None] * extended[None, :,...  18.8 us
    unnamed x117, local copies, waits for them, and re-layouts  14.5 us
    dot_general x1, matrix products, local(): lax.dot_general(spread.reshape(-1, BASES, channels), mixing, (((1, 2), (0...  12.2 us
  transfers between devices with their start and end apart: 10, of which 6 were waited for; matrix products, arithmetic and copies ran while one was open for 19% of the time, Pallas kernels for 0%

profile of v1, /device:TPU:8, one launch (start us, length us, event | category | flops | bytes accessed | tf_op | source)
XLA Modules:
  0.0 543.8 jit_solution(17689873148639645205)
XLA Ops:
  7.2 2.0 fusion.225
  9.2 1.7 collective-permute-start.1
  10.9 1.0 pad_dynamic-slice_fusion.6
  12.0 1.7 copy.254
  19.4 0.7 copy.232
  42.0 62.8 %all_gather.3 = f32[20,8,640]{0,1,2:T(8,128)S(1)} all-gather(f32[20,8,40]{0,1,2:T(8,128)} %copy.254), channel_id=1, replica_groups=mesh['ens'=16,'lon'=4,'lat'=4] {'ens'}, dimensions={2}, use_global_device_ids=true | all-gather | bytes 435200 | tf_op jit(solution)/shard_map/all_gather | solution.py:71
  104.8 1.7 copy.255
  106.5 3.5 collective-permute-start.2
  110.0 2.4 collective-permute-start.3
  113.3 3.5 collective-permute-done.3
  117.0 1.6 slice_bitcast_fusion.86
  119.1 3.3 slice_bitcast_fusion.62
  122.7 18.8 %multiply_add_fusion.1 = f32[7,1,20,8,640]{4,3,0,2,1:T(8,128)S(1)} fusion(f32[20,8,640]{2,1,0:T(8,128)} %get-tuple-element.68, f32[7,20]{0,1:T(8,128)S(1)} %copy-done.35, f32[20,8,640]{2,1,0:T(8,128)} %get-tuple-element.69, f32[7,20]{0,1:T(8,128)S(1)} %copy-done.36, f32[20,8,640]{2,1,0:T(8,128)} %get-tuple-element.70, f32[7,20]{0,1:T(8,128)S(1)} %copy-done.37, ...), kind=kLoop, calls=%fused_computation.104 | loop fusion | flops 69529600 | bytes 22965040 | tf_op jit(solution)/shard_map/add | solution.py:41
  141.6 8.1 %bitcast_subtract_fusion.3 = (f32[1,20,8,640]{3,2,1,0:T(8,128)S(1)}, f32[20,8,640]{2,1,0:T(8,128)S(1)}) fusion(f32[20,8,640]{2,1,0:T(8,128)S(1)} %copy-done.2, f32[1,20,8,640]{3,2,1,0:T(8,128)S(1)} %copy-done, f32[20,8,4480]{2,1,0:T(8,128)S(1)} %bitcast.466, f32[4480,640,1]{1,0,2:T(8,128)S(1)} %bitcast.463), kind=kOutput, calls=%fused_computation.331 | convolution fusion | flops 5505228800 | bytes 15974400 | tf_op jit(solution)/shard_map/dot_general | solution.py:63
  149.6 3.4 stack.4
  153.0 4.8 all-to-all-start
  159.8 135.7 %all-to-all-done = f32[16,1,20,8,640]{4,3,2,1,0:T(8,128)} async-done(((f32[16,1,20,8,640]{4,3,2,1,0:T(8,128)}), f32[16,1,20,8,640]{4,3,2,1,0:T(8,128)}, u32[]{:S(2)}, u32[]{:S(2)}) %all-to-all-start) | async-done | bytes 6553632 | tf_op jit(solution)/shard_map/all_to_all | solution.py:76
  295.5 6.2 %sqrt_reduce_fusion = (f32[20,8,640]{2,1,0:T(8,128)S(1)}, f32[20,8,640]{2,1,0:T(8,128)S(1)}) fusion(f32[16,1,20,8,640]{4,3,2,1,0:T(8,128)} %all-to-all-done, f32[20,8,640]{2,1,0:T(8,128)S(1)} %bitcast.468), kind=kLoop, calls=%fused_computation.3 | loop fusion | flops 9625600 | bytes 7782400 | tf_op jit(solution)/shard_map/reduce_sum | solution.py:81
  302.4 1.4 collective-permute-start.5
  323.4 4.9 copy.307
  328.3 5.6 %reshape.1464 = f32[640,160]{1,0:T(8,128)} reshape(f32[640,20,8]{2,1,0:T(8,128)} %bitcast.458) | data formatting | bytes 819200
  334.0 3.2 collective-permute-start.6
  337.2 2.7 collective-permute-start.7
  340.7 3.2 collective-permute-done.7
  344.2 3.2 slice_bitcast_fusion.20
  347.4 0.8 slice_bitcast_fusion.40
  348.3 3.9 slice_bitcast_fusion.41
  352.3 20.4 %fusion.231 = f32[20,8,7,640]{3,1,2,0:T(8,128)S(1)} fusion(f32[20,8,640]{2,1,0:T(8,128)} %get-tuple-element.26, f32[7,20]{0,1:T(8,128)} %copy.305, f32[20,8,640]{2,1,0:T(8,128)} %get-tuple-element.27, f32[7,20]{0,1:T(8,128)} %copy.304, f32[20,8,640]{2,1,0:T(8,128)} %get-tuple-element.28, f32[7,20]{0,1:T(8,128)} %copy.303, ...), kind=kLoop, calls=%fused_computation.6.clone.clone.clone.clone.clone.1 | loop fusion | flops 69529600 | bytes 22965040 | tf_op jit(solution)/shard_map/dot_general | solution.py:92
  372.7 12.2 %fusion.203 = f32[1,20,8,640]{3,2,1,0:T(8,128)} fusion(f32[7,640,640]{2,1,0:T(8,128)S(1)} %bitcast.465, f32[20,8,640]{2,1,0:T(8,128)S(1)} %copy-done.6, f32[1,20,8,640]{3,2,1,0:T(8,128)S(1)} %get-tuple-element.222, f32[20,8,7,640]{3,1,2,0:T(8,128)S(1)} %fusion.231), kind=kOutput, calls=%fused_computation.205 | convolution fusion | flops 5505638400 | bytes 15564800 | tf_op jit(solution)/shard_map/dot_general | solution.py:92
  384.9 150.1 %reduce-scatter.4.cloned.1.call-done = f32[40,160]{1,0:T(8,128)} async-done(((f32[640,160]{1,0:T(8,128)}), f32[40,160]{1,0:T(8,128)}) %reduce-scatter.4.cloned.1.call-update) | async-done | bytes 25616
  535.0 0.9 reshape.1465
  535.9 0.8 copy.308
  (251 shorter events, 52.4 us)
Async XLA Ops:
  9.1 97.3 %collective-permute-start = (f32[1,20,3,640]{3,2,1,0:T(4,128)}, f32[1,20,3,640]{3,2,1,0:T(4,128)S(1)}, u32[]{:S(2)}, u32[]{:S(2)}) collective-permute-start(f32[1,20,3,640]{3,2,1,0:T(4,128)} %get-tuple-element.116), channel_id=1, source_target_pairs={{0,4},{4,8},{8,12},{12,0},{1,5},{5,9},{9,13},{13,1},{2,6},{6,10},{... | collective-permute-start | bytes 460808 | tf_op jit(solution)/shard_map/ppermute | solution.py:19
  9.2 97.3 %collective-permute-start.1 = (f32[1,20,3,640]{3,2,1,0:T(4,128)}, f32[1,20,3,640]{3,2,1,0:T(4,128)S(1)}, u32[]{:S(2)}, u32[]{:S(2)}) collective-permute-start(f32[1,20,3,640]{3,2,1,0:T(4,128)} %get-tuple-element.117), channel_id=1, source_target_pairs={{4,0},{8,4},{12,8},{0,12},{5,1},{9,5},{13,9},{1,13},{6,2},{10,6},{... | collective-permute-start | bytes 460808 | tf_op jit(solution)/shard_map/ppermute | solution.py:22
  42.0 64.5 %copy-start = (f32[1,20,8,640]{3,2,1,0:T(8,128)S(1)}, f32[1,20,8,640]{3,2,1,0:T(8,128)}, u32[]{:S(2)}) copy-start(f32[1,20,8,640]{3,2,1,0:T(8,128)} %param.4) | copy-start | bytes 1228804
  106.5 6.8 %collective-permute-start.2 = (f32[1,3,14,640]{3,2,1,0:T(8,128)S(1)}, f32[1,3,14,640]{3,2,1,0:T(8,128)S(1)}, u32[]{:S(2)}, u32[]{:S(2)}) collective-permute-start(f32[1,3,14,640]{3,2,1,0:T(8,128)S(1)} %get-tuple-element.94), channel_id=1, source_target_pairs={{0,1},{1,2},{2,3},{4,5},{5,6},{6,7},{8,9},{9,10},{10,11},{12,13},{... | collective-permute-start | bytes 322568 | tf_op jit(solution)/shard_map/ppermute | solution.py:19
  110.0 6.8 %collective-permute-start.3 = (f32[1,3,14,640]{3,2,1,0:T(8,128)S(1)}, f32[1,3,14,640]{3,2,1,0:T(8,128)S(1)}, u32[]{:S(2)}, u32[]{:S(2)}) collective-permute-start(f32[1,3,14,640]{3,2,1,0:T(8,128)S(1)} %get-tuple-element.95), channel_id=1, source_target_pairs={{1,0},{2,1},{3,2},{5,4},{6,5},{7,6},{9,8},{10,9},{11,10},{13,12},{... | collective-permute-start | bytes 322568 | tf_op jit(solution)/shard_map/ppermute | solution.py:22
  118.7 3.6 copy-start.3
  118.7 3.6 copy-start.4
  118.7 3.6 copy-start.7
  118.7 3.6 copy-start.8
  118.8 3.6 copy-start.9
  118.8 3.6 copy-start.10
  122.3 19.2 %slice-start = ((s8[11468800]{0:T(1024)(128)(4,1)}), s8[4194304]{0:T(1024)(128)(4,1)S(1)}, s32[]{:S(2)}) async-start(s8[11468800]{0:T(1024)(128)(4,1)} %bitcast.461), calls=%async_computation.3 | async-start | bytes 8388608
  122.7 18.8 %slice-start.1 = ((s8[11468800]{0:T(1024)(128)(4,1)}), s8[4194304]{0:T(1024)(128)(4,1)S(1)}, s32[]{:S(2)}) async-start(s8[11468800]{0:T(1024)(128)(4,1)} %bitcast.461), calls=%async_computation.4 | async-start | bytes 8388608
  122.7 18.8 %slice-start.2 = ((s8[11468800]{0:T(1024)(128)(4,1)}), s8[3080192]{0:T(1024)(128)(4,1)S(1)}, s32[]{:S(2)}) async-start(s8[11468800]{0:T(1024)(128)(4,1)} %bitcast.461), calls=%async_computation.5 | async-start | bytes 6160384
  122.7 18.8 %copy-start.2 = (f32[20,8,640]{2,1,0:T(8,128)S(1)}, f32[20,8,640]{2,1,0:T(8,128)}, u32[]{:S(2)}) copy-start(f32[20,8,640]{2,1,0:T(8,128)} %copy.255) | copy-start | bytes 1228804
  153.0 5.0 copy-start.1
  153.0 142.5 %all-to-all-start = ((f32[16,1,20,8,640]{4,3,2,1,0:T(8,128)}), f32[16,1,20,8,640]{4,3,2,1,0:T(8,128)}, u32[]{:S(2)}, u32[]{:S(2)}) async-start(f32[16,1,20,8,640]{4,3,2,1,0:T(8,128)} %stack.4), calls=%async_computation | async-start | bytes 13107200 | tf_op jit(solution)/shard_map/all_to_all | solution.py:76
  157.8 377.2 %reduce-scatter.4.cloned.1.call-start = ((), (), s32[]{:S(2)}) async-start(), calls=%async_computation.2 | async-start | bytes 696320
  302.0 31.9 %collective-permute-start.4 = (f32[1,20,3,640]{3,2,1,0:T(4,128)S(1)}, f32[1,20,3,640]{3,2,1,0:T(4,128)S(1)}, u32[]{:S(2)}, u32[]{:S(2)}) collective-permute-start(f32[1,20,3,640]{3,2,1,0:T(4,128)S(1)} %get-tuple-element.113), channel_id=1, source_target_pairs={{0,4},{4,8},{8,12},{12,0},{1,5},{5,9},{9,13},{13,1},{2,6},{6,10},{... | collective-permute-start | bytes 460808 | tf_op jit(solution)/shard_map/ppermute | solution.py:19
  302.4 31.5 %collective-permute-start.5 = (f32[1,20,3,640]{3,2,1,0:T(4,128)S(1)}, f32[1,20,3,640]{3,2,1,0:T(4,128)S(1)}, u32[]{:S(2)}, u32[]{:S(2)}) collective-permute-start(f32[1,20,3,640]{3,2,1,0:T(4,128)S(1)} %get-tuple-element.114), channel_id=1, source_target_pairs={{4,0},{8,4},{12,8},{0,12},{5,1},{9,5},{13,9},{1,13},{6,2},{10,6},{... | collective-permute-start | bytes 460808 | tf_op jit(solution)/shard_map/ppermute | solution.py:22
  334.0 6.8 %collective-permute-start.6 = (f32[1,3,14,640]{3,2,1,0:T(8,128)S(1)}, f32[1,3,14,640]{3,2,1,0:T(8,128)S(1)}, u32[]{:S(2)}, u32[]{:S(2)}) collective-permute-start(f32[1,3,14,640]{3,2,1,0:T(8,128)S(1)} %get-tuple-element.90), channel_id=1, source_target_pairs={{0,1},{1,2},{2,3},{4,5},{5,6},{6,7},{8,9},{9,10},{10,11},{12,13},{... | collective-permute-start | bytes 322568 | tf_op jit(solution)/shard_map/ppermute | solution.py:19
  337.2 6.8 %collective-permute-start.7 = (f32[1,3,14,640]{3,2,1,0:T(8,128)S(1)}, f32[1,3,14,640]{3,2,1,0:T(8,128)S(1)}, u32[]{:S(2)}, u32[]{:S(2)}) collective-permute-start(f32[1,3,14,640]{3,2,1,0:T(8,128)S(1)} %get-tuple-element.91), channel_id=1, source_target_pairs={{1,0},{2,1},{3,2},{5,4},{6,5},{7,6},{9,8},{10,9},{11,10},{13,12},{... | collective-permute-start | bytes 322568 | tf_op jit(solution)/shard_map/ppermute | solution.py:22
  348.2 4.0 copy-start.15
  348.2 4.0 copy-start.17
  348.2 4.0 copy-start.19
  348.2 4.0 copy-start.21
  348.2 4.0 copy-start.23
  348.2 4.0 copy-start.25
  348.2 24.4 %slice-start.3 = ((s8[11468800]{0:T(1024)(128)(4,1)}), s8[3080192]{0:T(1024)(128)(4,1)S(1)}, s32[]{:S(2)}) async-start(s8[11468800]{0:T(1024)(128)(4,1)} %bitcast.464), calls=%async_computation.6 | async-start | bytes 6160384
  348.3 24.4 %slice-start.4 = ((s8[11468800]{0:T(1024)(128)(4,1)}), s8[4194304]{0:T(1024)(128)(4,1)S(1)}, s32[]{:S(2)}) async-start(s8[11468800]{0:T(1024)(128)(4,1)} %bitcast.464), calls=%async_computation.7 | async-start | bytes 8388608
  352.3 20.5 %slice-start.5 = ((s8[11468800]{0:T(1024)(128)(4,1)}), s8[4194304]{0:T(1024)(128)(4,1)S(1)}, s32[]{:S(2)}) async-start(s8[11468800]{0:T(1024)(128)(4,1)} %bitcast.464), calls=%async_computation.8 | async-start | bytes 8388608
  352.3 20.4 %copy-start.6 = (f32[20,8,640]{2,1,0:T(8,128)S(1)}, f32[20,8,640]{2,1,0:T(8,128)}, u32[]{:S(2)}) copy-start(f32[20,8,640]{2,1,0:T(8,128)} %copy-done.5) | copy-start | bytes 1228804
  (31 other events, 109.8 us)
Sparse Core Ops, SparseCore 0:
  334.0 200.9 reduce-scatter.3
